TPU v7x, 256 devices: a whole 4x4x8 slice. The times are simulated.
256 devices in a mesh: occ: 16 (over z, y_hi), aux: 16 (over y_lo, x, core).
Axes of the slice: x: 4, y: 4 (y_hi: 2, y_lo: 2; y = y_hi * 2 + y_lo), z: 8, core: 2. Of those that a mesh axis runs over, the one named last changes fastest.
Arguments:
- orbital_b: bfloat16 [128, 3072, 768], P('occ', 'aux'), may hold values from -0.75 to 0.75
- occ_energy: float32 [128], replicated, may hold values from -3 to -0.5
- vir_energy: float32 [768], replicated, may hold values from 0.2 to 3
Outputs:
- gradient_term: bfloat16 [128, 3072, 768], P('occ', 'aux')
All inputs are finite; a program needn't handle non-finite values.
Results may differ from a plain program's by a relative error of at most 0.0044.
Values may be sent and summed in bfloat16 or wider, within the bound.
A program may use at most 64 MiB of HBM per device.

v0:
```python
import jax
import jax.numpy as jnp
from jax import lax
from jax.sharding import PartitionSpec as P


def shifted(value, axis, steps):
    count = lax.axis_size(axis)
    initial, last = (max(0, -steps), min(count, count - steps))
    return lax.ppermute(value, axis, [(source, source + steps) for source in range(initial, last)])


def shards(orbital_b, occ_energy, vir_energy):
    occ_index = lax.axis_index("occ")
    aux_index = lax.axis_index("aux")
    occ_count = lax.axis_size("occ")
    block_rows = orbital_b.shape[0]
    vir_width = orbital_b.shape[2]
    slab_width = vir_width // lax.axis_size("aux")
    columns = lax.all_to_all(orbital_b, "aux", split_axis=2, concat_axis=1, tiled=True)
    own_energy = lax.dynamic_slice_in_dim(occ_energy, occ_index * block_rows, block_rows)
    vir_slab = lax.dynamic_slice_in_dim(vir_energy, aux_index * slab_width, slab_width)
    energy_left = occ_energy[jnp.maximum(occ_index - 1, 0) * block_rows]
    energy_right = occ_energy[jnp.minimum(occ_index + 1, occ_count - 1) * block_rows]
    partner_energy = jnp.stack([energy_left, energy_right])
    leading = columns[:1]
    from_left_block = shifted(leading, "occ", 1)
    from_right_block = shifted(leading, "occ", -1)
    partners = jnp.concatenate([from_left_block, from_right_block], axis=0)
    segment = lax.all_gather(partners, "aux", axis=2, tiled=True)
    integral = jnp.einsum("iPa,pPb->iapb", columns, segment, preferred_element_type=jnp.float32)
    denominator = (
        vir_slab[None, :, None, None]
        + vir_energy[None, None, None, :]
        - own_energy[:, None, None, None]
        - partner_energy[None, None, :, None]
    )
    amplitude = (integral / denominator).astype(jnp.bfloat16)
    running = jnp.einsum("iapb,pPb->iPa", amplitude, segment, preferred_element_type=jnp.float32)
    gradient_slab = running.astype(jnp.bfloat16)
    return lax.all_to_all(gradient_slab, "aux", split_axis=1, concat_axis=2, tiled=True)


def solution(mesh):
    placed = (P("occ", "aux", None), P(), P())
    return jax.shard_map(
        shards, mesh=mesh, in_specs=placed, out_specs=P("occ", "aux", None), check_vma=False
    )
```

profile of v0, /device:TPU:1, one launch (start us, length us, event | category | flops | bytes accessed | tf_op | source)
XLA Modules:
  0.0 229.1 jit_solution(18051163929910925184)
XLA Ops:
  6.5 5.0 %copy.15 = bf16[8,192,768]{1,0,2:T(8,128)(2,1)} copy(bf16[8,192,768]{2,1,0:T(8,128)(2,1)} %param.3) | data formatting | bytes 4718592 | tf_op args[0]
  11.6 44.4 %all_to_all.36 = bf16[8,192,768]{1,0,2:T(8,128)(2,1)S(1)} all-to-all(bf16[8,192,768]{1,0,2:T(8,128)(2,1)} %copy.15), channel_id=1, replica_groups=mesh['occ'=16,'aux'=16] {'aux'}, dimensions={2} | all-to-all | bytes 4718592 | tf_op jit(solution)/shard_map/all_to_all | solution.py:20
  55.9 0.6 copy.16
  56.7 0.1 copy.17
  56.8 1.1 slice.7
  57.9 1.3 collective-permute-start.1
  59.2 5.5 %collective-permute-start = (bf16[1,3072,48]{1,2,0:T(8,128)(2,1)}, bf16[1,3072,48]{1,2,0:T(8,128)(2,1)S(1)}, u32[]{:S(2)}, u32[]{:S(2)}) collective-permute-start(bf16[1,3072,48]{1,2,0:T(8,128)(2,1)} %slice.7), channel_id=1, source_target_pairs={{0,16},{16,32},{32,48},{48,64},{64,80},{80,96},{96,112},{112,128},... | collective-permute-start | bytes 884744 | tf_op jit(solution)/shard_map/ppermute | solution.py:10
  64.7 3.9 %collective-permute-done.1 = bf16[1,3072,48]{1,2,0:T(8,128)(2,1)S(1)} collective-permute-done((bf16[1,3072,48]{1,2,0:T(8,128)(2,1)}, bf16[1,3072,48]{1,2,0:T(8,128)(2,1)S(1)}, u32[]{:S(2)}, u32[]{:S(2)}) %collective-permute-start.1) | collective-permute-done | bytes 294944 | tf_op jit(solution)/shard_map/ppermute | solution.py:10
  68.6 8.0 %collective-permute-done = bf16[1,3072,48]{1,2,0:T(8,128)(2,1)S(1)} collective-permute-done((bf16[1,3072,48]{1,2,0:T(8,128)(2,1)}, bf16[1,3072,48]{1,2,0:T(8,128)(2,1)S(1)}, u32[]{:S(2)}, u32[]{:S(2)}) %collective-permute-start) | collective-permute-done | bytes 294944 | tf_op jit(solution)/shard_map/ppermute | solution.py:10
  76.6 0.9 pad_maximum_fusion
  77.7 0.6 fusion.15
  78.4 1.3 pad_maximum_fusion.1
  79.8 1.2 broadcast_subtract_fusion
  81.0 3.4 %copy.18 = bf16[8,16,192,48]{2,1,3,0:T(8,128)(2,1)} copy(bf16[8,16,192,48]{2,0,3,1:T(8,128)(2,1)S(1)} %bitcast.46) | data formatting | bytes 4718592 | tf_op jit(solution)/shard_map/all_to_all | solution.py:20
  84.4 5.1 %reshape.41 = bf16[8,3072,48,1]{1,2,0,3:T(8,128)(2,1)S(1)} reshape(bf16[8,16,192,48]{2,1,3,0:T(8,128)(2,1)} %copy.18) | data formatting | bytes 4718592 | tf_op jit(solution)/shard_map/all_to_all | solution.py:20
  89.5 50.5 %all-gather.2.cloned.1.call-done = bf16[2,3072,768]{1,2,0:T(8,128)(2,1)} async-done(((bf16[2,3072,48]{1,2,0:T(8,128)(2,1)}), bf16[2,3072,768]{1,2,0:T(8,128)(2,1)}) %all-gather.2.cloned.1.call-update) | async-done | bytes 9437200 | tf_op jit(solution)/shard_map/all_gather | solution.py:30
  140.0 8.0 %fusion.9 = bf16[8,48,2,768]{3,1,2,0:T(8,128)(2,1)S(1)} fusion(bf16[8,3072,48,1]{1,2,0,3:T(8,128)(2,1)S(1)} %reshape.41, bf16[2,3072,768]{1,2,0:T(8,128)(2,1)} %all-gather.2.cloned.1.call-done, f32[2]{0:T(128)S(1)} %pad_maximum_fusion.1, f32[8,48,768]{2,1,0:T(8,128)} %broadcast_subtract_fusion), kind=kOutput, calls=%fused_computation.7 | convolution fusion | flops 3625648128 | bytes 14155784 | tf_op jit(solution)/shard_map/iPa,pPb->iapb/dot_general | solution.py:31
  148.0 4.2 %fusion.6 = bf16[8,3072,48]{1,2,0:T(8,128)(2,1)S(1)} fusion(bf16[8,48,2,768]{3,1,2,0:T(8,128)(2,1)S(1)} %fusion.9, bf16[2,3072,768]{1,2,0:T(8,128)(2,1)S(1)} %copy-done.2), kind=kOutput, calls=%fused_computation.5 | convolution fusion | flops 3625058304 | bytes 12976128 | tf_op jit(solution)/shard_map/iapb,pPb->iPa/dot_general | solution.py:39
  152.1 6.0 %copy.19 = bf16[8,3072,48]{2,0,1:T(8,128)(2,1)} copy(bf16[8,3072,48]{1,2,0:T(8,128)(2,1)S(1)} %fusion.6) | data formatting | bytes 4718592 | tf_op jit(solution)/shard_map/convert_element_type | solution.py:40
  158.1 10.3 %reshape.44 = bf16[16,2,36864]{2,1,0:T(2,128)(2,1)S(1)} reshape(bf16[3072,8,48]{2,1,0:T(8,128)(2,1)} %bitcast.48) | data formatting | bytes 4718592
  168.4 34.7 %all_to_all.37 = bf16[16,2,36864]{2,1,0:T(2,128)(2,1)} all-to-all(bf16[16,2,36864]{2,1,0:T(2,128)(2,1)S(1)} %reshape.44), channel_id=1, replica_groups=mesh['occ'=16,'aux'=16] {'aux'}, dimensions={0} | all-to-all | bytes 4718592 | tf_op jit(solution)/shard_map/all_to_all | solution.py:41
  203.2 9.2 %reshape.45 = bf16[3072,8,48]{2,1,0:T(8,128)(2,1)} reshape(bf16[16,2,36864]{2,1,0:T(2,128)(2,1)} %all_to_all.37) | data formatting | bytes 4718592
  212.4 7.2 %copy.20 = bf16[8,16,192,48]{2,3,1,0:T(8,128)(2,1)S(1)} copy(bf16[8,16,192,48]{3,0,2,1:T(8,128)(2,1)} %bitcast.47) | data formatting | bytes 4718592 | tf_op jit(solution)/shard_map/all_to_all | solution.py:41
  219.6 2.6 %copy.21 = bf16[8,192,768]{2,1,0:T(8,128)(2,1)} copy(bf16[8,192,768]{1,2,0:T(8,128)(2,1)S(1)} %bitcast.49) | data formatting | bytes 4718592 | tf_op jit(solution)/shard_map/all_to_all | solution.py:41
  (12 shorter events, 0.3 us)
Async XLA Ops:
  6.5 133.4 %all-gather.2.cloned.1.call-start = ((), (), s32[]{:S(2)}) async-start(), calls=%async_computation.2 | async-start | bytes 10027008 | tf_op jit(solution)/shard_map/all_gather | solution.py:30
  56.6 21.0 %copy-start.1 = (f32[128]{0:T(128)S(1)}, f32[128]{0:T(128)}, u32[]{:S(2)}) copy-start(f32[128]{0:T(128)} %param.4) | copy-start | bytes 1540
  56.6 21.0 %copy-start = (f32[768]{0:T(1024)S(1)}, f32[768]{0:T(1024)}, u32[]{:S(2)}) copy-start(f32[768]{0:T(1024)} %param.5) | copy-start | bytes 9220
  57.9 10.7 %collective-permute-start.1 = (bf16[1,3072,48]{1,2,0:T(8,128)(2,1)}, bf16[1,3072,48]{1,2,0:T(8,128)(2,1)S(1)}, u32[]{:S(2)}, u32[]{:S(2)}) collective-permute-start(bf16[1,3072,48]{1,2,0:T(8,128)(2,1)} %slice.7), channel_id=1, source_target_pairs={{16,0},{32,16},{48,32},{64,48},{80,64},{96,80},{112,96},{128,112},... | collective-permute-start | bytes 884744 | tf_op jit(solution)/shard_map/ppermute | solution.py:10
  59.2 17.5 %collective-permute-start = (bf16[1,3072,48]{1,2,0:T(8,128)(2,1)}, bf16[1,3072,48]{1,2,0:T(8,128)(2,1)S(1)}, u32[]{:S(2)}, u32[]{:S(2)}) collective-permute-start(bf16[1,3072,48]{1,2,0:T(8,128)(2,1)} %slice.7), channel_id=1, source_target_pairs={{0,16},{16,32},{32,48},{48,64},{64,80},{80,96},{96,112},{112,128},... | collective-permute-start | bytes 884744 | tf_op jit(solution)/shard_map/ppermute | solution.py:10
  140.0 8.0 %copy-start.2 = (bf16[2,3072,768]{1,2,0:T(8,128)(2,1)S(1)}, bf16[2,3072,768]{1,2,0:T(8,128)(2,1)}, u32[]{:S(2)}) copy-start(bf16[2,3072,768]{1,2,0:T(8,128)(2,1)} %all-gather.2.cloned.1.call-done) | copy-start | bytes 28311556
Sparse Core Ops, SparseCore 0:
  77.7 62.2 all-gather.1
where the time goes:
time: 230 us; the launch traced here: 229 us
  blocking collectives  79.1 us (34%)
  waiting for transfers between devices  62.5 us (27%)
  local copies, waits for them, and re-layouts  51.5 us (22%)
  between operations  13.5 us (6%)
  matrix products  12.1 us (5%)
  starting transfers between devices  6.79 us (3%)
  other arithmetic  3.49 us (2%)
    all_gather x1, waiting for transfers between devices, shards(): segment = lax.all_gather(partners, 'aux', axis=2, tiled=True)  50.5 us
    all_to_all x1, blocking collectives, shards(): lax.all_to_all(orbital_b, 'aux', split_axis=2, concat_axis=1, tiled=True)  44.4 us
    all_to_all x1, blocking collectives, shards(): lax.all_to_all(gradient_slab, 'aux', split_axis=1, concat_axis=2, tiled=T...  34.7 us
    unnamed x9, local copies, waits for them, and re-layouts  24.6 us
    ppermute x2, waiting for transfers between devices, shifted(): lax.ppermute(value, axis, [(source, source + steps) for source in range(i...  12 us
    all_to_all x2, local copies, waits for them, and re-layouts, shards(): lax.all_to_all(gradient_slab, 'aux', split_axis=1, concat_axis=2, tiled=T...  9.8 us
    all_to_all x3, local copies, waits for them, and re-layouts, shards(): lax.all_to_all(orbital_b, 'aux', split_axis=2, concat_axis=1, tiled=True)  9.12 us
    dot_general x1, matrix products, shards(): jnp.einsum('iPa,pPb->iapb', columns, segment, preferred_element_type=jnp....  7.96 us
  transfers between devices with their start and end apart: 3, of which 3 were waited for; matrix products, arithmetic and copies ran while one was open for 5% of the time, Pallas kernels for 0%

commit v1 on v0

v1 whole, which is shorter than its diff:
```python
import functools

import jax
import jax.numpy as jnp
from jax import lax
from jax.experimental import pallas as pl
from jax.experimental.pallas import tpu as pltpu
from jax.sharding import PartitionSpec as P

MESH = pl.DeviceIdType.MESH
OFFSETS = ((0, 1), (0, 3), (1, 0), (0, 2), (1, 1), (1, 3), (1, 2))
ALONG_X = (1, 3, 2)
CHUNKS = 3


def kernel(planes, occ_e, vir, b_own, out, part, amp, gam, lead, b_in, b_t, integral, p_out, p_in,
           ls, lr, bs, br, ps, pr, as_, ar, gs, gr, local):
    rows, width = b_own.shape[1], b_own.shape[2]
    w = width // CHUNKS
    half = w // 2
    occ, aux = lax.axis_index("occ"), lax.axis_index("aux")
    z, yh = occ // 2, occ % 2
    yl, x, h = aux // 8, (aux // 2) % 4, aux % 2
    me = yl * 4 + x

    def device(z_to, yh_to, yl_to, x_to, h_to):
        return (lax.rem(z_to + planes, planes) * 2 + yh_to, (yl_to * 4 + x_to) * 2 + h_to)

    def chip(dy, dx):
        return lax.rem(yl + dy, 2), lax.rem(x + dx, 4)

    def send(src, dst, ssem, rsem, to):
        copy = pltpu.make_async_remote_copy(
            src_ref=src, dst_ref=dst, send_sem=ssem, recv_sem=rsem, device_id=to, device_id_type=MESH)
        copy.start()
        return copy

    step = 1 - 2 * yh
    twins = (device(z + step, yh, yl, x, h), device(z - step, yh, yl, x, h))
    mate = device(z, yh, yl, x, 1 - h)
    peers = []
    for dy, dx in OFFSETS:
        yp, xp = chip(dy, dx)
        peers.append(device(z, yh, yp, xp, h))
    sources = (device(z, 1 - yh, 0, x, h), device(z - step, 1 - yh, 1, x, h))
    z_col = z - yl * step
    columns = (device(z_col, 1 - yh, 0, x, h), device(z_col, 1 - yh, 1, x, h))

    barrier = pltpu.get_barrier_semaphore()
    for to in (*peers, mate, *twins, *sources):
        pl.semaphore_signal(barrier, inc=1, device_id=to, device_id_type=MESH)
    pl.semaphore_wait(barrier, 12)

    def span(c):
        return pl.ds(pl.multiple_of(c * rows, rows), rows)

    def cols(q):
        return pl.ds(q * w, w)

    waits = []

    def send_b(q):
        for n, (dy, dx) in enumerate(OFFSETS):
            yp, xp = chip(dy, dx)
            waits.append(send(b_own.at[yp * 4 + xp, :, cols(q)], b_in.at[span(me), cols(q)],
                              bs.at[q, n], br.at[q, n], peers[n]))

    for n in range(2):
        waits.append(send(b_own.at[0], lead.at[yl, span(me)], ls.at[0, n], lr.at[yl, 0], columns[n]))
    mine = pltpu.make_async_copy(b_own.at[me], b_in.at[span(me)], local.at[0])
    mine.start()
    send_b(0)

    def arrived(ref, sem):
        pltpu.make_async_copy(ref, ref, sem).wait()

    def piece(s, r):
        d = (0, *ALONG_X)[r]
        return s * 4 + lax.rem(x - d + 4, 4)

    for s in range(2):
        c = piece(s, 0)
        held = lead.at[s, span(c)]
        arrived(held, lr.at[s, 0])
        for n, d in enumerate(ALONG_X):
            waits.append(send(held, held, ls.at[1 + s, n], lr.at[s, 1 + n],
                              device(z, yh, yl, lax.rem(x + d, 4), h)))
        waits.append(send(held, lead.at[1 - s, span(c)], ls.at[3 + s, 0], lr.at[1 - s, 4], twins[s]))
    send_b(1)
    for r in range(1, 4):
        for s in range(2):
            c = piece(s, r)
            held = lead.at[s, span(c)]
            arrived(held, lr.at[s, r])
            waits.append(send(held, lead.at[1 - s, span(c)], ls.at[3 + s, r], lr.at[1 - s, 4 + r], twins[s]))
    send_b(2)
    mine.wait()
    for r in range(4):
        for s in range(2):
            arrived(lead.at[1 - s, span(piece(s, r))], lr.at[1 - s, 4 + r])

    z_b = z - step
    valid = jnp.where(jnp.logical_and(z_b >= 0, z_b < planes), 1.0, 0.0).astype(jnp.float32)
    block_b = jnp.clip(z_b, 0, planes - 1) * 2 + 1 - yh
    e_own = occ_e[occ * 8 + me]
    e_pair = (occ_e[(z * 2 + 1 - yh) * 8], occ_e[block_b * 8])

    own = pl.ds(pl.multiple_of(h * half, half), half)
    other = pl.ds(pl.multiple_of((1 - h) * half, half), half)

    def partial(q):
        for n, (dy, dx) in enumerate(OFFSETS):
            yp, xp = chip(-dy + 2, -dx + 4)
            arrived(b_in.at[span(yp * 4 + xp), cols(q)], br.at[q, n])
        b_t[...] = b_in[:, cols(q)].T
        for s in range(2):
            integral[:, s * width:(s + 1) * width] = jnp.dot(
                b_t[...], lead[s], preferred_element_type=jnp.float32)
        p_out[q] = integral[other, :].astype(jnp.bfloat16)
        waits.append(send(p_out.at[q], p_in.at[q], ps.at[q], pr.at[q], mate))

    def amplitude(q):
        arrived(p_in.at[q], pr.at[q])
        row = vir[0:1, pl.ds(pl.multiple_of(q * w + h * half, 128), half)]
        va = jnp.broadcast_to(row, (half, half)).T
        for s in range(2):
            for t in range(width // half):
                at = pl.ds(s * width + t * half, half)
                total = integral[own, at] + p_in[q, :, at].astype(jnp.float32)
                if s == 1:
                    total = total * valid
                low = va + vir[0:1, pl.ds(t * half, half)] - e_own - e_pair[s]
                amp[q, own, at] = (total / low).astype(jnp.bfloat16)
        waits.append(send(amp.at[q, own], amp.at[q, own], as_.at[q], ar.at[q], mate))

    def gamma(q):
        arrived(amp.at[q, other], ar.at[q])

        def one(c):
            acc = jnp.zeros((rows, w), jnp.float32)
            for s in range(2):
                acc += lax.dot_general(lead[s, span(c), :], amp[q, :, s * width:(s + 1) * width],
                                       (((1,), (1,)), ((), ())), preferred_element_type=jnp.float32)
            gam[q, span(c), :] = acc.astype(jnp.bfloat16)

        for n, (dy, dx) in enumerate(OFFSETS):
            yp, xp = chip(dy, dx)
            c = yp * 4 + xp
            one(c)
            waits.append(send(gam.at[q, span(c)], out.at[me, :, cols(q)], gs.at[q, n], gr.at[q, n], peers[n]))
        one(me)
        copy = pltpu.make_async_copy(gam.at[q, span(me)], out.at[me, :, cols(q)], local.at[1 + q])
        copy.start()
        return copy

    copies = []
    for q in range(CHUNKS):
        partial(q)
        amplitude(q)
        copies.append(gamma(q))

    for copy in waits:
        copy.wait_send()
    for copy in copies:
        copy.wait()
    for q in range(CHUNKS):
        for n, (dy, dx) in enumerate(OFFSETS):
            yp, xp = chip(-dy + 2, -dx + 4)
            arrived(out.at[yp * 4 + xp, :, cols(q)], gr.at[q, n])


def solution(mesh):
    planes = mesh.shape["occ"] // 2

    def shards(orbital_b, occ_energy, vir_energy):
        orbitals, rows, width = orbital_b.shape
        w = width // CHUNKS
        aux = orbitals * rows
        dma = pltpu.SemaphoreType.DMA
        bf16, f32 = jnp.bfloat16, jnp.float32
        result = pl.pallas_call(
            functools.partial(kernel, planes),
            out_shape=jax.ShapeDtypeStruct(orbital_b.shape, orbital_b.dtype),
            in_specs=[pl.BlockSpec(memory_space=pltpu.SMEM), pl.BlockSpec(memory_space=pltpu.VMEM),
                      pl.BlockSpec(memory_space=pl.ANY)],
            out_specs=pl.BlockSpec(memory_space=pl.ANY),
            scratch_shapes=[
                pltpu.VMEM((8, 128), f32),
                pltpu.VMEM((CHUNKS, w, 2 * width), bf16),
                pltpu.VMEM((CHUNKS, aux, w), bf16),
                pltpu.VMEM((2, aux, width), bf16),
                pltpu.VMEM((aux, width), bf16),
                pltpu.VMEM((w, aux), bf16),
                pltpu.VMEM((w, 2 * width), f32),
                pltpu.VMEM((CHUNKS, w // 2, 2 * width), bf16),
                pltpu.VMEM((CHUNKS, w // 2, 2 * width), bf16),
                dma((5, 4)), dma((2, 8)), dma((CHUNKS, 7)), dma((CHUNKS, 7)),
                dma((CHUNKS,)), dma((CHUNKS,)), dma((CHUNKS,)), dma((CHUNKS,)),
                dma((CHUNKS, 7)), dma((CHUNKS, 7)), dma((1 + CHUNKS,)),
            ],
            compiler_params=pltpu.CompilerParams(
                collective_id=0, has_side_effects=True, vmem_limit_bytes=48 * 2**20),
        )(occ_energy, vir_energy.reshape(1, -1), orbital_b)
        return result

    placed = (P("occ", "aux", None), P(), P())
    return jax.shard_map(
        shards, mesh=mesh, in_specs=placed, out_specs=P("occ", "aux", None), check_vma=False)
```

time: 230 us -> 106 us (0.46)
  Pallas kernels: 0 us -> 99.8 us
  blocking collectives: 79.1 us -> 0 us
  waiting for transfers between devices: 62.5 us -> 0 us
  local copies, waits for them, and re-layouts: 51.5 us -> 4.42 us
  between operations: 13.5 us -> 0.01 us
  matrix products: 12.1 us -> 0 us
  starting transfers between devices: 6.79 us -> 0 us
  other arithmetic: 3.49 us -> 0 us
    pallas_call x0 -> x1, Pallas kernels: none -> 99.8 us  [shards(): pl.pallas_call(functools.partial(kernel, planes), out_shape=jax.ShapeDtyp...]
    all_to_all x2 -> x0, blocking collectives: 79.1 us -> none  [the longest x1 44.4 us: shards(): lax.all_to_all(orbital_b, 'aux', split_axis=2, concat_axis=1, tiled=True)]
    all_gather x1 -> x0, waiting for transfers between devices: 50.5 us -> none  [shards(): segment = lax.all_gather(partners, 'aux', axis=2, tiled=True)]
    unnamed x9 -> x5, local copies, waits for them, and re-layouts: 24.6 us -> 3.73 us
    all_to_all x5 -> x0, local copies, waits for them, and re-layouts: 18.9 us -> none  [the longest x2 9.8 us: shards(): lax.all_to_all(gradient_slab, 'aux', split_axis=1, concat_axis=2, tiled=T...]
    dot_general x2 -> x0, matrix products: 12.1 us -> none  [the longest x1 7.96 us: shards(): jnp.einsum('iPa,pPb->iapb', columns, segment, preferred_element_type=jnp....]
    ppermute x2 -> x0, waiting for transfers between devices: 12 us -> none  [shifted(): lax.ppermute(value, axis, [(source, source + steps) for source in range(i...]
    ppermute x2 -> x0, starting transfers between devices: 6.79 us -> none  [shifted(): lax.ppermute(value, axis, [(source, source + steps) for source in range(i...]
  transfers between devices with their start and end apart: 3 -> 0, of which waited for: 3 -> 0; matrix products, arithmetic and copies ran while one was open for 5% -> 0% of each run, Pallas kernels for 0% -> 0%
where the time goes in v1:
time: 106 us; the launch traced here: 104 us
  Pallas kernels  99.8 us (94%)
  local copies, waits for them, and re-layouts  4.42 us (4%)
    pallas_call x1, Pallas kernels, shards(): pl.pallas_call(functools.partial(kernel, planes), out_shape=jax.ShapeDtyp...  99.8 us
    unnamed x5, local copies, waits for them, and re-layouts  3.73 us

profile of v1, /device:TPU:1, one launch (start us, length us, event | category | flops | bytes accessed | tf_op | source)
XLA Modules:
  0.0 104.2 jit_solution(17973894406523795335)
XLA Ops:
  0.0 0.7 reshape.3.vir
  0.7 0.0 copy-start
  0.7 1.7 %copy-done = bf16[8,192,768]{2,1,0:T(8,128)(2,1)S(1)} copy-done((bf16[8,192,768]{2,1,0:T(8,128)(2,1)S(1)}, bf16[8,192,768]{2,1,0:T(8,128)(2,1)}, u32[]{:S(2)}) %copy-start) | copy-done | bytes 2359320
  2.4 0.0 copy-start.1
  2.4 0.7 copy-done.1
  3.0 99.8 %shard_map.37 = bf16[8,192,768]{2,1,0:T(8,128)(2,1)S(1)} custom-call(f32[128]{0:T(128)S(1)} %copy-done.1, f32[1,768]{1,0:T(1,128)S(1)} %reshape.3.vir, bf16[8,192,768]{2,1,0:T(8,128)(2,1)S(1)} %copy-done), custom_call_target="tpu_custom_call" | custom-call | tf_op jit(solution)/shard_map/pallas_call | solution.py:181
  102.8 1.4 %copy.5 = bf16[8,192,768]{2,1,0:T(8,128)(2,1)} copy(bf16[8,192,768]{2,1,0:T(8,128)(2,1)S(1)} %shard_map.37) | data formatting | bytes 4718592
Async XLA Ops:
  0.7 1.7 %copy-start = (bf16[8,192,768]{2,1,0:T(8,128)(2,1)S(1)}, bf16[8,192,768]{2,1,0:T(8,128)(2,1)}, u32[]{:S(2)}) copy-start(bf16[8,192,768]{2,1,0:T(8,128)(2,1)} %b_own.1) | copy-start | bytes 7077892
  2.4 0.7 copy-start.1

commit v2 on v1

v2 whole, which is shorter than its diff:
```python
import functools

import jax
import jax.numpy as jnp
from jax import lax
from jax.experimental import pallas as pl
from jax.experimental.pallas import tpu as pltpu
from jax.sharding import PartitionSpec as P

MESH = pl.DeviceIdType.MESH
OFFSETS = ((0, 1), (0, 3), (1, 0), (1, 1), (1, 3), (0, 2), (1, 2))
ALONG_X = (1, 3, 2)
CHUNKS = 3
PARTS = 4


def kernel(planes, occ_hbm, vir_hbm, b_own, out, occ_e, vir, vrow, scale, amp, gam, lead, b_in, b_t, integral,
           p_out, p_in, ls, lr, bs, br, ps, pr, as_, ar, gs, gr, local):
    rows, width = b_own.shape[1], b_own.shape[2]
    w = width // CHUNKS
    half = w // 2
    occ, aux = lax.axis_index("occ"), lax.axis_index("aux")
    z, yh = occ // 2, occ % 2
    yl, x, h = aux // 8, (aux // 2) % 4, aux % 2
    me = yl * 4 + x

    def device(z_to, yh_to, yl_to, x_to, h_to):
        return (lax.rem(z_to + planes, planes) * 2 + yh_to, (yl_to * 4 + x_to) * 2 + h_to)

    def chip(dy, dx):
        return lax.rem(yl + dy, 2), lax.rem(x + dx, 4)

    def send(src, dst, ssem, rsem, to):
        copy = pltpu.make_async_remote_copy(
            src_ref=src, dst_ref=dst, send_sem=ssem, recv_sem=rsem, device_id=to, device_id_type=MESH)
        copy.start()
        return copy

    step = 1 - 2 * yh
    twins = (device(z + step, yh, yl, x, h), device(z - step, yh, yl, x, h))
    mate = device(z, yh, yl, x, 1 - h)
    across = device(z, yh, 1 - yl, x, h)
    beside = [device(z, yh, yl, lax.rem(x + d, 4), h) for d in ALONG_X]
    far = (1 - yl) * 4 + x
    peers = []
    for dy, dx in OFFSETS:
        yp, xp = chip(dy, dx)
        peers.append(device(z, yh, yp, xp, h))
    column = device(z - yl * step, 1 - yh, 1 - yl, x, h)
    source = device(z - (1 - yl) * step, 1 - yh, 1 - yl, x, h)

    occ_in = pltpu.make_async_copy(occ_hbm, occ_e, local.at[1])
    vir_in = pltpu.make_async_copy(vir_hbm, vir, local.at[2])
    occ_in.start()
    vir_in.start()
    barrier = pltpu.get_barrier_semaphore()
    for to in (*peers, mate, *twins, source):
        pl.semaphore_signal(barrier, inc=1, device_id=to, device_id_type=MESH)
    pl.semaphore_wait(barrier, 11)

    def span(c):
        return pl.ds(pl.multiple_of(c * rows, rows), rows)

    def cols(q):
        return pl.ds(q * w, w)

    waits = []

    def send_b(q, which):
        for n in which:
            dy, dx = OFFSETS[n]
            yp, xp = chip(dy, dx)
            waits.append(send(b_own.at[yp * 4 + xp, :, cols(q)], b_in.at[span(me), cols(q)],
                              bs.at[q, n], br.at[q, n], peers[n]))

    def b_wait(q):
        for n, (dy, dx) in enumerate(OFFSETS):
            yp, xp = chip(-dy + 2, -dx + 4)
            arrived(b_in.at[span(yp * 4 + xp), cols(q)], br.at[q, n])

    fine = rows // PARTS

    def sub(c, t):
        return pl.ds(pl.multiple_of(c * rows + t * fine, fine), fine)

    def arrived(ref, sem):
        pltpu.make_async_copy(ref, ref, sem).wait()

    def piece(s, r):
        d = (0, *ALONG_X)[r]
        return s * 4 + lax.rem(x - d + 4, 4)

    def forward_x(s, c, t):
        held = lead.at[s, sub(c, t)]
        for n in range(2):
            waits.append(send(held, held, ls.at[1 + s, n, t], lr.at[s, 1 + n, t], beside[n]))

    def forward_z(s, c, r, t):
        to = device(z + (1 - 2 * s) * step, yh, yl, x, h)
        waits.append(send(lead.at[s, sub(c, t)], lead.at[1 - s, sub(c, t)], ls.at[3 + s, r, t],
                          lr.at[1 - s, 4 + r, t], to))

    z_b = z - step
    valid = jnp.where(jnp.logical_and(z_b >= 0, z_b < planes), 1.0, 0.0).astype(jnp.float32)
    block_b = jnp.clip(z_b, 0, planes - 1) * 2 + 1 - yh

    own = pl.ds(pl.multiple_of(h * half, half), half)
    other = pl.ds(pl.multiple_of((1 - h) * half, half), half)

    def scales(q):
        e_own = occ_e[occ * 8 + me]
        e_pair = (occ_e[(z * 2 + 1 - yh) * 8], occ_e[block_b * 8])
        va = jnp.broadcast_to(vrow[0:1, pl.ds(pl.multiple_of(q * w + h * half, 128), half)], (half, half)).T
        for s in range(2):
            for t in range(width // half):
                low = va + vrow[0:1, pl.ds(t * half, half)] - e_own - e_pair[s]
                scale[q, :, pl.ds(s * width + t * half, half)] = (valid if s else 1.0) / low

    for t in range(PARTS):
        waits.append(send(b_own.at[0, pl.ds(t * fine, fine)], lead.at[yl, sub(me, t)],
                          ls.at[0, 0, t], lr.at[yl, 0, t], column))
    send_b(0, range(3))
    mine = pltpu.make_async_copy(b_own.at[me], b_in.at[span(me)], local.at[0])
    mine.start()

    occ_in.wait()
    vir_in.wait()
    for t in range(width // half):
        vrow[0:1, pl.ds(t * half, half)] = vir[pl.ds(t * half, half)].reshape(1, half)

    for t in range(PARTS + 2):
        if t < PARTS:
            first = lead.at[1 - yl, sub(far, t)]
            arrived(first, lr.at[1 - yl, 0, t])
            waits.append(send(first, first, ls.at[0, 1, t], lr.at[1 - yl, 0, t], across))
            forward_x(1 - yl, far, t)
            forward_z(1 - yl, far, 0, t)
            arrived(lead.at[yl, sub(me, t)], lr.at[yl, 0, t])
            forward_x(yl, me, t)
            forward_z(yl, me, 0, t)
        if t < CHUNKS:
            scales(t)
        if t == PARTS - 1:
            send_b(0, range(3, 7))
        for r, lag in ((1, 1), (2, 1), (3, 2)):
            if r == 3 and t == PARTS:
                for q in range(1, CHUNKS):
                    send_b(q, range(7))
            if 0 <= t - lag < PARTS:
                u = t - lag
                for s in range(2):
                    c = piece(s, r)
                    arrived(lead.at[s, sub(c, u)], lr.at[s, r, u])
                    if r - 1 == u % 2:
                        held = lead.at[s, sub(c, u)]
                        waits.append(send(held, held, ls.at[1 + s, 2, u], lr.at[s, 3, u], beside[r - 1]))
                    forward_z(s, c, r, u)
    mine.wait()
    for t in range(PARTS):
        for r in range(4):
            for s in range(2):
                arrived(lead.at[1 - s, sub(piece(s, r), t)], lr.at[1 - s, 4 + r, t])

    def partial(q):
        b_wait(q)
        b_t[...] = b_in[:, cols(q)].T
        for s in range(2):
            integral[:, s * width:(s + 1) * width] = jnp.dot(
                b_t[...], lead[s], preferred_element_type=jnp.float32)
        p_out[q] = integral[other, :].astype(jnp.bfloat16)
        waits.append(send(p_out.at[q], p_in.at[q], ps.at[q], pr.at[q], mate))

    def amplitude(q):
        arrived(p_in.at[q], pr.at[q])
        for s in range(2):
            at = pl.ds(s * width, width)
            total = integral[own, at] + p_in[q, :, at].astype(jnp.float32)
            amp[q, own, at] = (total * scale[q, :, at]).astype(jnp.bfloat16)
        waits.append(send(amp.at[q, own], amp.at[q, own], as_.at[q], ar.at[q], mate))

    def gamma(q):
        arrived(amp.at[q, other], ar.at[q])

        def one(c):
            acc = jnp.zeros((rows, w), jnp.float32)
            for s in range(2):
                acc += lax.dot_general(lead[s, span(c), :], amp[q, :, s * width:(s + 1) * width],
                                       (((1,), (1,)), ((), ())), preferred_element_type=jnp.float32)
            gam[q, span(c), :] = acc.astype(jnp.bfloat16)

        for n, (dy, dx) in enumerate(OFFSETS):
            yp, xp = chip(dy, dx)
            c = yp * 4 + xp
            one(c)
            waits.append(send(gam.at[q, span(c)], out.at[me, :, cols(q)], gs.at[q, n], gr.at[q, n], peers[n]))
        one(me)
        copy = pltpu.make_async_copy(gam.at[q, span(me)], out.at[me, :, cols(q)], local.at[3 + q])
        copy.start()
        return copy

    copies = []
    partial(0)
    amplitude(0)
    copies.append(gamma(0))
    partial(1)
    for q in range(1, CHUNKS):
        amplitude(q)
        if q + 1 < CHUNKS:
            partial(q + 1)
        copies.append(gamma(q))

    for copy in waits:
        copy.wait_send()
    for copy in copies:
        copy.wait()
    for q in range(CHUNKS):
        for n, (dy, dx) in enumerate(OFFSETS):
            yp, xp = chip(-dy + 2, -dx + 4)
            arrived(out.at[yp * 4 + xp, :, cols(q)], gr.at[q, n])


def solution(mesh):
    planes = mesh.shape["occ"] // 2

    def shards(orbital_b, occ_energy, vir_energy):
        orbitals, rows, width = orbital_b.shape
        w = width // CHUNKS
        aux = orbitals * rows
        dma = pltpu.SemaphoreType.DMA
        bf16, f32 = jnp.bfloat16, jnp.float32
        result = pl.pallas_call(
            functools.partial(kernel, planes),
            out_shape=jax.ShapeDtypeStruct(orbital_b.shape, orbital_b.dtype),
            in_specs=[pl.BlockSpec(memory_space=pltpu.MemorySpace.HBM)] * 3,
            out_specs=pl.BlockSpec(memory_space=pl.ANY),
            scratch_shapes=[
                pltpu.SMEM(occ_energy.shape, f32),
                pltpu.VMEM(vir_energy.shape, f32),
                pltpu.VMEM((8, width), f32),
                pltpu.VMEM((CHUNKS, w // 2, 2 * width), f32),
                pltpu.VMEM((CHUNKS, w, 2 * width), bf16),
                pltpu.VMEM((CHUNKS, aux, w), bf16),
                pltpu.VMEM((2, aux, width), bf16),
                pltpu.VMEM((aux, width), bf16),
                pltpu.VMEM((w, aux), bf16),
                pltpu.VMEM((w, 2 * width), f32),
                pltpu.VMEM((CHUNKS, w // 2, 2 * width), bf16),
                pltpu.VMEM((CHUNKS, w // 2, 2 * width), bf16),
                dma((5, 4, PARTS)), dma((2, 8, PARTS)), dma((CHUNKS, 7)), dma((CHUNKS, 7)),
                dma((CHUNKS,)), dma((CHUNKS,)), dma((CHUNKS,)), dma((CHUNKS,)),
                dma((CHUNKS, 7)), dma((CHUNKS, 7)), dma((3 + CHUNKS,)),
            ],
            compiler_params=pltpu.CompilerParams(
                collective_id=0, has_side_effects=True, vmem_limit_bytes=48 * 2**20),
        )(occ_energy, vir_energy, orbital_b)
        return result

    placed = (P("occ", "aux", None), P(), P())
    return jax.shard_map(
        shards, mesh=mesh, in_specs=placed, out_specs=P("occ", "aux", None), check_vma=False)
```

time: 106 us -> 94.4 us (0.89); the launches traced: 104 us -> 94.3 us
  Pallas kernels: 99.8 us -> 89.9 us
    pallas_call x1, Pallas kernels: 99.8 us -> 89.9 us  [shards(): pl.pallas_call(functools.partial(kernel, planes), out_shape=jax.ShapeDtyp...]
    unnamed x5 -> x7, local copies, waits for them, and re-layouts: 3.73 us -> 4.41 us
where the time goes in v2:
time: 94.4 us; the launch traced here: 94.3 us
  Pallas kernels  89.9 us (95%)
  local copies, waits for them, and re-layouts  4.41 us (5%)
    pallas_call x1, Pallas kernels, shards(): pl.pallas_call(functools.partial(kernel, planes), out_shape=jax.ShapeDtyp...  89.9 us
    unnamed x7, local copies, waits for them, and re-layouts  4.41 us

profile of v2, /device:TPU:1, one launch (start us, length us, event | category | flops | bytes accessed | tf_op | source)
XLA Modules:
  0.0 94.3 jit_solution(17060822801320323006)
XLA Ops:
  0.0 0.0 copy-start
  0.0 1.7 %copy-done = bf16[8,192,768]{2,1,0:T(8,128)(2,1)S(1)} copy-done((bf16[8,192,768]{2,1,0:T(8,128)(2,1)S(1)}, bf16[8,192,768]{2,1,0:T(8,128)(2,1)}, u32[]{:S(2)}) %copy-start) | copy-done | bytes 2359320
  1.7 0.0 copy-start.1
  1.7 0.7 copy-done.1
  2.4 0.0 copy-start.2
  2.4 0.7 copy-done.2
  3.0 89.9 %shard_map.37 = bf16[8,192,768]{2,1,0:T(8,128)(2,1)S(1)} custom-call(f32[128]{0:T(128)S(1)} %copy-done.2, f32[768]{0:T(1024)S(1)} %copy-done.1, bf16[8,192,768]{2,1,0:T(8,128)(2,1)S(1)} %copy-done), custom_call_target="tpu_custom_call" | custom-call | tf_op jit(solution)/shard_map/pallas_call | solution.py:231
  92.9 1.4 %copy.5 = bf16[8,192,768]{2,1,0:T(8,128)(2,1)} copy(bf16[8,192,768]{2,1,0:T(8,128)(2,1)S(1)} %shard_map.37) | data formatting | bytes 4718592
Async XLA Ops:
  0.0 1.7 %copy-start = (bf16[8,192,768]{2,1,0:T(8,128)(2,1)S(1)}, bf16[8,192,768]{2,1,0:T(8,128)(2,1)}, u32[]{:S(2)}) copy-start(bf16[8,192,768]{2,1,0:T(8,128)(2,1)} %b_own.1) | copy-start | bytes 7077892
  1.7 0.7 copy-start.1
  2.4 0.7 copy-start.2

commit v3 on v2

--- a/solution.py
+++ b/solution.py
@@ -8,13 +8,13 @@
 from jax.sharding import PartitionSpec as P
 
 MESH = pl.DeviceIdType.MESH
-OFFSETS = ((0, 1), (0, 3), (1, 0), (1, 1), (1, 3), (0, 2), (1, 2))
+OFFSETS = ((0, 1), (0, 3), (1, 0), (0, 2), (1, 1), (1, 3), (1, 2))
 ALONG_X = (1, 3, 2)
 CHUNKS = 3
 PARTS = 4
 
 
-def kernel(planes, occ_hbm, vir_hbm, b_own, out, occ_e, vir, vrow, scale, amp, gam, lead, b_in, b_t, integral,
+def kernel(planes, occ_hbm, vir_hbm, b_own, out, occ_e, vir, vrow, vcol, scale, amp, gam, lead, b_in, b_t, integral,
            p_out, p_in, ls, lr, bs, br, ps, pr, as_, ar, gs, gr, local):
     rows, width = b_own.shape[1], b_own.shape[2]
     w = width // CHUNKS
@@ -25,7 +25,10 @@
     me = yl * 4 + x
 
     def device(z_to, yh_to, yl_to, x_to, h_to):
-        return (lax.rem(z_to + planes, planes) * 2 + yh_to, (yl_to * 4 + x_to) * 2 + h_to)
+        return (z_to * 2 + yh_to, (yl_to * 4 + x_to) * 2 + h_to)
+
+    def within(z_to):
+        return jnp.logical_and(z_to >= 0, z_to < planes)
 
     def chip(dy, dx):
         return lax.rem(yl + dy, 2), lax.rem(x + dx, 4)
@@ -37,7 +40,17 @@
         return copy
 
     step = 1 - 2 * yh
-    twins = (device(z + step, yh, yl, x, h), device(z - step, yh, yl, x, h))
+
+    def twin(s):
+        z_to = z + (1 - 2 * s) * step
+        inside = within(z_to)
+        return device(jnp.where(inside, z_to, z), jnp.where(inside, yh, 1 - yh), jnp.where(inside, yl, 1 - yl), x, h)
+
+    def entry(z_to):
+        inside = within(z_to)
+        return device(jnp.where(inside, z_to, z), jnp.where(inside, 1 - yh, yh), 1 - yl, x, h)
+
+    twins = (twin(0), twin(1))
     mate = device(z, yh, yl, x, 1 - h)
     across = device(z, yh, 1 - yl, x, h)
     beside = [device(z, yh, yl, lax.rem(x + d, 4), h) for d in ALONG_X]
@@ -46,8 +59,8 @@
     for dy, dx in OFFSETS:
         yp, xp = chip(dy, dx)
         peers.append(device(z, yh, yp, xp, h))
-    column = device(z - yl * step, 1 - yh, 1 - yl, x, h)
-    source = device(z - (1 - yl) * step, 1 - yh, 1 - yl, x, h)
+    column = entry(z - yl * step)
+    source = entry(z - (1 - yl) * step)
 
     occ_in = pltpu.make_async_copy(occ_hbm, occ_e, local.at[1])
     vir_in = pltpu.make_async_copy(vir_hbm, vir, local.at[2])
@@ -96,12 +109,12 @@
             waits.append(send(held, held, ls.at[1 + s, n, t], lr.at[s, 1 + n, t], beside[n]))
 
     def forward_z(s, c, r, t):
-        to = device(z + (1 - 2 * s) * step, yh, yl, x, h)
+        to = twin(s)
         waits.append(send(lead.at[s, sub(c, t)], lead.at[1 - s, sub(c, t)], ls.at[3 + s, r, t],
                           lr.at[1 - s, 4 + r, t], to))
 
     z_b = z - step
-    valid = jnp.where(jnp.logical_and(z_b >= 0, z_b < planes), 1.0, 0.0).astype(jnp.float32)
+    valid = jnp.where(within(z_b), 1.0, 0.0).astype(jnp.float32)
     block_b = jnp.clip(z_b, 0, planes - 1) * 2 + 1 - yh
 
     own = pl.ds(pl.multiple_of(h * half, half), half)
@@ -110,23 +123,29 @@
     def scales(q):
         e_own = occ_e[occ * 8 + me]
         e_pair = (occ_e[(z * 2 + 1 - yh) * 8], occ_e[block_b * 8])
-        va = jnp.broadcast_to(vrow[0:1, pl.ds(pl.multiple_of(q * w + h * half, 128), half)], (half, half)).T
+        for u in range(w // 128):
+            column_of = jnp.broadcast_to(vrow[0:1, pl.ds(q * w + u * 128, 128)], (128, 128))
+            vcol[pl.ds(u * 128, 128), :] = column_of.T
+        va = vcol[own, :]
         for s in range(2):
-            for t in range(width // half):
-                low = va + vrow[0:1, pl.ds(t * half, half)] - e_own - e_pair[s]
-                scale[q, :, pl.ds(s * width + t * half, half)] = (valid if s else 1.0) / low
-
-    for t in range(PARTS):
+            for t in range(width // 128):
+                low = va + vrow[0:1, pl.ds(t * 128, 128)] - e_own - e_pair[s]
+                scale[q, :, pl.ds(s * width + t * 128, 128)] = (valid if s else 1.0) / low
+
+    def enter(t):
         waits.append(send(b_own.at[0, pl.ds(t * fine, fine)], lead.at[yl, sub(me, t)],
                           ls.at[0, 0, t], lr.at[yl, 0, t], column))
+
+    enter(0)
+    enter(1)
     send_b(0, range(3))
     mine = pltpu.make_async_copy(b_own.at[me], b_in.at[span(me)], local.at[0])
     mine.start()
 
     occ_in.wait()
     vir_in.wait()
-    for t in range(width // half):
-        vrow[0:1, pl.ds(t * half, half)] = vir[pl.ds(t * half, half)].reshape(1, half)
+    for t in range(width // 128):
+        vrow[0:1, pl.ds(t * 128, 128)] = vir[pl.ds(t * 128, 128)].reshape(1, 128)
 
     for t in range(PARTS + 2):
         if t < PARTS:
@@ -138,6 +157,8 @@
             arrived(lead.at[yl, sub(me, t)], lr.at[yl, 0, t])
             forward_x(yl, me, t)
             forward_z(yl, me, 0, t)
+        if t + 2 < PARTS:
+            enter(t + 2)
         if t < CHUNKS:
             scales(t)
         if t == PARTS - 1:
@@ -237,6 +258,7 @@
                 pltpu.SMEM(occ_energy.shape, f32),
                 pltpu.VMEM(vir_energy.shape, f32),
                 pltpu.VMEM((8, width), f32),
+                pltpu.VMEM((w, 128), f32),
                 pltpu.VMEM((CHUNKS, w // 2, 2 * width), f32),
                 pltpu.VMEM((CHUNKS, w, 2 * width), bf16),
                 pltpu.VMEM((CHUNKS, aux, w), bf16),
@@ -252,7 +274,7 @@
             ],
             compiler_params=pltpu.CompilerParams(
                 collective_id=0, has_side_effects=True, vmem_limit_bytes=48 * 2**20),
-        )(occ_energy, vir_energy, orbital_b)
+        )(*(pltpu.with_memory_space_constraint(v, pltpu.MemorySpace.HBM) for v in (occ_energy, vir_energy, orbital_b)))
         return result
 
     placed = (P("occ", "aux", None), P(), P())

time: 94.4 us -> 90 us (0.953)
  local copies, waits for them, and re-layouts: 4.41 us -> 1.41 us
  Pallas kernels: 89.9 us -> 88.5 us
    unnamed x7 -> x1, local copies, waits for them, and re-layouts: 4.41 us -> 1.41 us
    pallas_call x1, Pallas kernels: 89.9 us -> 88.5 us  [shards(): pl.pallas_call(functools.partial(kernel, planes), out_shape=jax.ShapeDtyp...]
where the time goes in v3:
time: 90 us; the launch traced here: 89.9 us
  Pallas kernels  88.5 us (98%)
  local copies, waits for them, and re-layouts  1.41 us (2%)
    pallas_call x1, Pallas kernels, shards(): pl.pallas_call(functools.partial(kernel, planes), out_shape=jax.ShapeDtyp...  88.5 us

profile of v3, /device:TPU:1, one launch (start us, length us, event | category | flops | bytes accessed | tf_op | source)
XLA Modules:
  0.0 89.9 jit_solution(570078235704078292)
XLA Ops:
  0.0 88.5 %shard_map.37 = bf16[8,192,768]{2,1,0:T(8,128)(2,1)S(1)} custom-call(f32[128]{0:T(128)} %occ_hbm.1, f32[768]{0:T(1024)} %vir_hbm.1, bf16[8,192,768]{2,1,0:T(8,128)(2,1)} %b_own.1), custom_call_target="tpu_custom_call" | custom-call | tf_op jit(solution)/shard_map/pallas_call | solution.py:252
  88.5 1.4 %copy.5 = bf16[8,192,768]{2,1,0:T(8,128)(2,1)} copy(bf16[8,192,768]{2,1,0:T(8,128)(2,1)S(1)} %shard_map.37) | data formatting | bytes 4718592

commit v4 on v3

--- a/solution.py
+++ b/solution.py
@@ -138,7 +138,7 @@
 
     enter(0)
     enter(1)
-    send_b(0, range(3))
+    send_b(0, range(4))
     mine = pltpu.make_async_copy(b_own.at[me], b_in.at[span(me)], local.at[0])
     mine.start()
 
@@ -162,7 +162,7 @@
         if t < CHUNKS:
             scales(t)
         if t == PARTS - 1:
-            send_b(0, range(3, 7))
+            send_b(0, range(4, 7))
         for r, lag in ((1, 1), (2, 1), (3, 2)):
             if r == 3 and t == PARTS:
                 for q in range(1, CHUNKS):

time: 90 us -> 88.2 us (0.980)
  Pallas kernels: 88.5 us -> 86.5 us
    pallas_call x1, Pallas kernels: 88.5 us -> 86.5 us  [shards(): pl.pallas_call(functools.partial(kernel, planes), out_shape=jax.ShapeDtyp...]
where the time goes in v4:
time: 88.2 us; the launch traced here: 87.9 us
  Pallas kernels  86.5 us (98%)
  local copies, waits for them, and re-layouts  1.41 us (2%)
    pallas_call x1, Pallas kernels, shards(): pl.pallas_call(functools.partial(kernel, planes), out_shape=jax.ShapeDtyp...  86.5 us

profile of v4, /device:TPU:1, one launch (start us, length us, event | category | flops | bytes accessed | tf_op | source)
XLA Modules:
  0.0 87.9 jit_solution(8571411993674103181)
XLA Ops:
  0.0 86.5 %shard_map.37 = bf16[8,192,768]{2,1,0:T(8,128)(2,1)S(1)} custom-call(f32[128]{0:T(128)} %occ_hbm.1, f32[768]{0:T(1024)} %vir_hbm.1, bf16[8,192,768]{2,1,0:T(8,128)(2,1)} %b_own.1), custom_call_target="tpu_custom_call" | custom-call | tf_op jit(solution)/shard_map/pallas_call | solution.py:252
  86.5 1.4 %copy.5 = bf16[8,192,768]{2,1,0:T(8,128)(2,1)} copy(bf16[8,192,768]{2,1,0:T(8,128)(2,1)S(1)} %shard_map.37) | data formatting | bytes 4718592
